TPU v7x, 512 devices: a whole 4x4x16 slice. The times are simulated.
512 devices in a mesh: dp: 16 (over z), expert: 32 (over x, y, core).
Axes of the slice: x: 4, y: 4, z: 16, core: 2. Of those that a mesh axis runs over, the one named last changes fastest.
Arguments:
- first_out: bfloat16 [65536, 1024], P(('dp', 'expert')), may hold values from -6 to 6
- second_out: bfloat16 [65536, 1024], P(('dp', 'expert')), may hold values from -6 to 6
- first_grad: bfloat16 [65536, 1024], P(('dp', 'expert')), may hold values from -6 to 6
- second_grad: bfloat16 [65536, 1024], P(('dp', 'expert')), may hold values from -6 to 6
- routes: int32 [65536, 2], P(('dp', 'expert')), may hold values from 0 to 31, all different within a row; in each aligned block of 128 rows (0 to 127, 128 to 255, ...) at most 16 rows name the same one
- gate_values: float32 [65536, 2], P(('dp', 'expert')), may hold values from 0.1 to 1
- w_gate: bfloat16 [32, 1024, 768], P('expert', 'dp'), may hold values from -0.1875 to 0.1875
- w_up: bfloat16 [32, 1024, 768], P('expert', 'dp'), may hold values from -0.1875 to 0.1875
- w_down: bfloat16 [32, 1024, 768], P('expert', 'dp'), may hold values from -0.21875 to 0.21875
Outputs:
- second_in: bfloat16 [65536, 1024], P(('dp', 'expert'))
- first_total: bfloat16 [65536, 1024], P(('dp', 'expert'))
- gate_grad: float32 [65536, 2], P(('dp', 'expert'))
- w_down_grad: float32 [32, 1024, 768], P('expert', 'dp')
Inputs may be any that keep to these rules, and one draw needn't show every extreme that they name: `routes`: each row names 2 different experts. Among the 128 rows of one device no expert is named more than 16 times, and in every draw some device names some expert exactly 16 times.
All inputs are finite; a program needn't handle non-finite values.
Results may differ from a plain program's by a relative error of at most 0.0051.
Values may be sent and summed in bfloat16 or wider, within the bound.
No kernel may reach another device: no remote copies, remote signals or barrier semaphores. Data moves between devices by JAX's collectives and lax.ppermute only.
A program may use at most 64 MiB of HBM per device.

v0:
```python
import math
import jax
import jax.numpy as jnp
from jax import lax
from jax.sharding import PartitionSpec as P


def expert_rows(rows_in, rows_cot, gate_mat, up_mat, down_mat):
    pre_gate = jnp.dot(rows_in, gate_mat, preferred_element_type=jnp.float32)
    pre_up = jnp.dot(rows_in, up_mat, preferred_element_type=jnp.float32)
    squashed = jax.nn.sigmoid(pre_gate)
    activated = pre_gate * squashed
    hidden = (activated * pre_up).astype(jnp.bfloat16)
    out_rows = lax.dot_general(
        hidden, down_mat, (((1,), (1,)), ((), ())), preferred_element_type=jnp.float32
    ).astype(jnp.bfloat16)
    hidden_cot = jnp.dot(rows_cot, down_mat, preferred_element_type=jnp.float32)
    gate_cot = (hidden_cot * pre_up * squashed * (1.0 + pre_gate * (1.0 - squashed))).astype(
        jnp.bfloat16
    )
    up_cot = (hidden_cot * activated).astype(jnp.bfloat16)
    input_cot = lax.dot_general(
        gate_cot, gate_mat, (((1,), (1,)), ((), ())), preferred_element_type=jnp.float32
    )
    input_cot = input_cot + lax.dot_general(
        up_cot, up_mat, (((1,), (1,)), ((), ())), preferred_element_type=jnp.float32
    )
    return (out_rows, input_cot.astype(jnp.bfloat16), hidden)


def to_slots(placing, assigned_rows):
    return lax.dot_general(
        placing, assigned_rows, (((0,), (0,)), ((), ())), preferred_element_type=jnp.float32
    ).astype(jnp.bfloat16)


def per_device(
    first_out, second_out, first_grad, second_grad, routes, gate_values, w_gate, w_up, w_down
):
    count_here = first_out.shape[0]
    feature_count = first_out.shape[1]
    top_count = routes.shape[1]
    owners = lax.axis_size("expert")
    groups = lax.axis_size("dp")
    capacity = min(count_here, 2 * count_here * top_count // owners)
    assigned = count_here * top_count
    slots_all = owners * capacity
    expert_ids = routes.reshape(assigned)
    onehot = (expert_ids[:, None] == jnp.arange(owners, dtype=jnp.int32)[None, :]).astype(jnp.int32)
    before = jnp.cumsum(onehot, axis=0) - onehot
    rank_in = jnp.sum(before * onehot, axis=1)
    slot_index = expert_ids * capacity + rank_in
    placing = (slot_index[:, None] == jnp.arange(slots_all, dtype=jnp.int32)[None, :]).astype(
        jnp.bfloat16
    )
    repeated = jnp.broadcast_to(
        first_out[:, None, :], (count_here, top_count, feature_count)
    ).reshape(assigned, feature_count)
    grad_repeated = jnp.broadcast_to(
        second_grad[:, None, :], (count_here, top_count, feature_count)
    ).reshape(assigned, feature_count)
    cot_rows = (gate_values.reshape(assigned)[:, None] * grad_repeated.astype(jnp.float32)).astype(
        jnp.bfloat16
    )
    send_input = to_slots(placing, repeated).reshape(owners, capacity, feature_count)
    send_cot = to_slots(placing, cot_rows).reshape(owners, capacity, feature_count)
    arrived_input, arrived_cot = (
        lax.all_to_all(send_input, "expert", split_axis=0, concat_axis=0, tiled=True),
        lax.all_to_all(send_cot, "expert", split_axis=0, concat_axis=0, tiled=True),
    )
    rows_in = arrived_input.reshape(slots_all, feature_count)
    rows_cot = arrived_cot.reshape(slots_all, feature_count)
    hidden_count = w_gate.shape[2]
    shards = jnp.concatenate([w_gate[0], w_up[0], w_down[0]], axis=1)
    mats = lax.all_gather(shards, "dp", axis=0, tiled=True)
    gate_mat = mats[:, :hidden_count]
    up_mat = mats[:, hidden_count : 2 * hidden_count]
    down_mat = mats[:, 2 * hidden_count :]
    out_rows, input_cot, hidden = expert_rows(rows_in, rows_cot, gate_mat, up_mat, down_mat)
    grad_scale = 1.0 / math.sqrt(count_here * groups)
    partial_grad = lax.dot_general(
        rows_cot, hidden, (((0,), (0,)), ((), ())), preferred_element_type=jnp.float32
    )
    reduced = lax.psum_scatter(partial_grad, "dp", scatter_dimension=0, tiled=True)
    w_down_grad = (reduced * grad_scale)[None]
    back_out, back_cot = (
        lax.all_to_all(
            out_rows.reshape(owners, capacity, feature_count),
            "expert",
            split_axis=0,
            concat_axis=0,
            tiled=True,
        ),
        lax.all_to_all(
            input_cot.reshape(owners, capacity, feature_count),
            "expert",
            split_axis=0,
            concat_axis=0,
            tiled=True,
        ),
    )
    out_assigned = jnp.dot(
        placing, back_out.reshape(slots_all, feature_count), preferred_element_type=jnp.float32
    )
    cot_assigned = jnp.dot(
        placing, back_cot.reshape(slots_all, feature_count), preferred_element_type=jnp.float32
    )
    expert_out = out_assigned.reshape(count_here, top_count, feature_count)
    combined = jnp.sum(gate_values[:, :, None] * expert_out, axis=1)
    second_in = (second_out.astype(jnp.float32) - combined).astype(jnp.bfloat16)
    gate_grad = jnp.sum(second_grad.astype(jnp.float32)[:, None, :] * expert_out, axis=2)
    first_total = (
        first_grad.astype(jnp.float32)
        + jnp.sum(cot_assigned.reshape(count_here, top_count, feature_count), axis=1)
    ).astype(jnp.bfloat16)
    return (second_in, first_total, gate_grad, w_down_grad)


def solution(mesh):
    placed = (
        P(("dp", "expert"), None),
        P(("dp", "expert"), None),
        P(("dp", "expert"), None),
        P(("dp", "expert"), None),
        P(("dp", "expert"), None),
        P(("dp", "expert"), None),
        P("expert", "dp", None),
        P("expert", "dp", None),
        P("expert", "dp", None),
    )
    return jax.shard_map(
        per_device,
        mesh=mesh,
        in_specs=placed,
        out_specs=(
            P(("dp", "expert"), None),
            P(("dp", "expert"), None),
            P(("dp", "expert"), None),
            P("expert", "dp", None),
        ),
        check_vma=False,
    )
```

profile of v0, /device:TPU:2, one launch (start us, length us, event | category | flops | bytes accessed | tf_op | source)
XLA Modules:
  0.0 185.1 jit_solution(12592394571378709768)
XLA Ops:
  7.2 1.7 pad_maximum_fusion
  9.0 0.8 copy.21
  10.1 0.6 reduce-window.6
  10.7 0.2 slice_reduce_fusion
  10.9 1.2 broadcast_in_dim.6
  12.1 0.2 reshape.109
  12.4 1.5 convolution_convert_fusion.2
  14.0 9.5 %all-to-all-start = ((bf16[32,16,1024]{2,1,0:T(8,128)(2,1)}), bf16[32,16,1024]{2,1,0:T(8,128)(2,1)S(1)}, u32[]{:S(2)}, u32[]{:S(2)}) async-start(bf16[32,16,1024]{2,1,0:T(8,128)(2,1)} %bitcast.2), calls=%async_computation | async-start | bytes 2097152 | tf_op jit(solution)/shard_map/all_to_all | solution.py:68
  23.5 0.3 broadcast_in_dim.7.clone
  23.8 0.7 convert_element_type.61
  24.8 1.6 convolution_convert_fusion.1
  26.4 11.6 %all-to-all-done = bf16[32,16,1024]{2,1,0:T(8,128)(2,1)S(1)} async-done(((bf16[32,16,1024]{2,1,0:T(8,128)(2,1)}), bf16[32,16,1024]{2,1,0:T(8,128)(2,1)S(1)}, u32[]{:S(2)}, u32[]{:S(2)}) %all-to-all-start) | async-done | bytes 1048608 | tf_op jit(solution)/shard_map/all_to_all | solution.py:68
  38.0 6.4 %all-to-all-start.2 = ((bf16[32,16,1024]{2,1,0:T(8,128)(2,1)}), bf16[32,16,1024]{2,1,0:T(8,128)(2,1)S(1)}, u32[]{:S(2)}, u32[]{:S(2)}) async-start(bf16[32,16,1024]{2,1,0:T(8,128)(2,1)} %bitcast.10), calls=%async_computation.2 | async-start | bytes 2097152 | tf_op jit(solution)/shard_map/all_to_all | solution.py:69
  44.4 49.0 %all-gather.2.cloned.1.call-done = bf16[1024,2304]{1,0:T(8,128)(2,1)} async-done(((bf16[64,2304]{1,0:T(8,128)(2,1)}), bf16[1024,2304]{1,0:T(8,128)(2,1)}) %all-gather.2.cloned.1.call-update) | async-done | bytes 4718608 | tf_op jit(solution)/shard_map/all_gather | solution.py:75
  93.5 2.4 %fusion.9 = f32[512,768]{1,0:T(8,128)S(1)} fusion(bf16[512,1024]{1,0:T(8,128)(2,1)S(1)} %bitcast.53, bf16[1024,2304]{1,0:T(8,128)(2,1)} %all-gather.2.cloned.1.call-done), kind=kOutput, calls=%fused_computation.17 | convolution fusion | flops 805306368 | bytes 4194304 | tf_op jit(solution)/shard_map/dot_general | solution.py:9
  95.9 1.2 copy-done.5
  97.0 3.6 %multiply_convert_fusion.2 = (bf16[512,768]{1,0:T(8,128)(2,1)S(1)}, f32[512,768]{1,0:T(8,128)}) fusion(f32[512,768]{1,0:T(8,128)S(1)} %fusion.9, bf16[512,1024]{1,0:T(8,128)(2,1)S(1)} %bitcast.54, bf16[1024,2304]{1,0:T(8,128)(2,1)} %all-gather.2.cloned.1.call-done), kind=kOutput, calls=%fused_computation.3 | convolution fusion | flops 807665664 | bytes 6553600 | tf_op jit(solution)/shard_map/dot_general | solution.py:10
  100.7 2.7 %fusion.27 = f32[1024,768]{1,0:T(8,128)} fusion(bf16[512,1024]{1,0:T(8,128)(2,1)S(1)} %bitcast.51, bf16[512,768]{1,0:T(8,128)(2,1)S(1)} %get-tuple-element.6), kind=kOutput, calls=%fused_computation.49 | convolution fusion | flops 805306368 | bytes 4980736 | tf_op jit(solution)/shard_map/dot_general | solution.py:81
  103.4 2.5 %fusion.1 = f32[512,768]{1,0:T(8,128)S(1)} fusion(bf16[512,1024]{1,0:T(8,128)(2,1)S(1)} %bitcast.52, bf16[1024,2304]{1,0:T(8,128)(2,1)} %all-gather.2.cloned.1.call-done), kind=kOutput, calls=%fused_computation.9 | convolution fusion | flops 805306368 | bytes 4194304 | tf_op jit(solution)/shard_map/dot_general | solution.py:17
  106.0 2.9 %fusion.7 = f32[512,1024]{1,0:T(8,128)S(1)} fusion(bf16[1024,2304]{1,0:T(8,128)(2,1)} %all-gather.2.cloned.1.call-done, f32[512,768]{1,0:T(8,128)S(1)} %copy-done.6, f32[512,768]{1,0:T(8,128)S(1)} %fusion.1, f32[512,768]{1,0:T(8,128)S(1)} %copy-done.7), kind=kOutput, calls=%fused_computation.15 | convolution fusion | flops 809238528 | bytes 8388608 | tf_op jit(solution)/shard_map/dot_general | solution.py:22
  108.8 3.5 %add_convert_fusion = bf16[512,1024]{1,0:T(8,128)(2,1)} fusion(f32[512,1024]{1,0:T(8,128)S(1)} %fusion.7, bf16[1024,2304]{1,0:T(8,128)(2,1)} %all-gather.2.cloned.1.call-done, f32[512,768]{1,0:T(8,128)S(1)} %fusion.1, f32[512,768]{1,0:T(8,128)S(1)} %copy-done.6), kind=kOutput, calls=%fused_computation | convolution fusion | flops 808714240 | bytes 7864320 | tf_op jit(solution)/shard_map/dot_general | solution.py:25
  112.3 7.7 %all-to-all-start.3 = ((bf16[32,16,1024]{2,1,0:T(8,128)(2,1)}), bf16[32,16,1024]{2,1,0:T(8,128)(2,1)S(1)}, u32[]{:S(2)}, u32[]{:S(2)}) async-start(bf16[32,16,1024]{2,1,0:T(8,128)(2,1)} %bitcast.12), calls=%async_computation.3 | async-start | bytes 2097152 | tf_op jit(solution)/shard_map/all_to_all | solution.py:94
  120.1 3.5 %convolution_convert_fusion = bf16[512,1024]{1,0:T(8,128)(2,1)} fusion(bf16[512,768]{1,0:T(8,128)(2,1)S(1)} %get-tuple-element.6, bf16[1024,2304]{1,0:T(8,128)(2,1)} %all-gather.2.cloned.1.call-done), kind=kOutput, calls=%fused_computation.6 | convolution fusion | flops 805830656 | bytes 3407872 | tf_op jit(solution)/shard_map/dot_general | solution.py:14
  123.5 10.9 %all-to-all-done.3 = bf16[32,16,1024]{2,1,0:T(8,128)(2,1)S(1)} async-done(((bf16[32,16,1024]{2,1,0:T(8,128)(2,1)}), bf16[32,16,1024]{2,1,0:T(8,128)(2,1)S(1)}, u32[]{:S(2)}, u32[]{:S(2)}) %all-to-all-start.3) | async-done | bytes 1048608 | tf_op jit(solution)/shard_map/all_to_all | solution.py:94
  134.5 6.4 %all-to-all-start.1 = ((bf16[32,16,1024]{2,1,0:T(8,128)(2,1)}), bf16[32,16,1024]{2,1,0:T(8,128)(2,1)S(1)}, u32[]{:S(2)}, u32[]{:S(2)}) async-start(bf16[32,16,1024]{2,1,0:T(8,128)(2,1)} %bitcast.7), calls=%async_computation.1 | async-start | bytes 2097152 | tf_op jit(solution)/shard_map/all_to_all | solution.py:87
  141.2 0.5 convolution_reduce_fusion
  141.7 13.6 %all-to-all-done.1 = bf16[32,16,1024]{2,1,0:T(8,128)(2,1)S(1)} async-done(((bf16[32,16,1024]{2,1,0:T(8,128)(2,1)}), bf16[32,16,1024]{2,1,0:T(8,128)(2,1)S(1)}, u32[]{:S(2)}, u32[]{:S(2)}) %all-to-all-start.1) | async-done | bytes 1048608 | tf_op jit(solution)/shard_map/all_to_all | solution.py:87
  155.3 1.1 multiply_reduce_fusion
  156.5 0.8 add_convert_fusion.1
  157.2 0.8 subtract_convert_fusion
  158.0 18.7 %reduce-scatter.2.cloned.1.call-done = f32[64,768]{1,0:T(8,128)} async-done(((f32[1024,768]{1,0:T(8,128)}), f32[64,768]{1,0:T(8,128)}) %reduce-scatter.2.cloned.1.call-update) | async-done | bytes 196624 | tf_op jit(solution)/shard_map/reduce_scatter | solution.py:84
  176.7 1.6 multiply_bitcast_fusion
  (33 shorter events, 1.1 us)
Async XLA Ops:
  7.2 86.3 %all-gather.2.cloned.1.call-start = ((), (), s32[]{:S(2)}) async-start(), calls=%async_computation.5 | async-start | bytes 5013504 | tf_op jit(solution)/shard_map/all_gather | solution.py:75
  12.4 11.1 %copy-start = (bf16[128,1024]{1,0:T(8,128)(2,1)S(1)}, bf16[128,1024]{1,0:T(8,128)(2,1)}, u32[]{:S(2)}) copy-start(bf16[128,1024]{1,0:T(8,128)(2,1)} %param.12) | copy-start | bytes 786436
  14.0 24.0 %all-to-all-start = ((bf16[32,16,1024]{2,1,0:T(8,128)(2,1)}), bf16[32,16,1024]{2,1,0:T(8,128)(2,1)S(1)}, u32[]{:S(2)}, u32[]{:S(2)}) async-start(bf16[32,16,1024]{2,1,0:T(8,128)(2,1)} %bitcast.2), calls=%async_computation | async-start | bytes 2097152 | tf_op jit(solution)/shard_map/all_to_all | solution.py:68
  23.5 1.0 copy-start.4
  38.0 62.7 %all-to-all-start.2 = ((bf16[32,16,1024]{2,1,0:T(8,128)(2,1)}), bf16[32,16,1024]{2,1,0:T(8,128)(2,1)S(1)}, u32[]{:S(2)}, u32[]{:S(2)}) async-start(bf16[32,16,1024]{2,1,0:T(8,128)(2,1)} %bitcast.10), calls=%async_computation.2 | async-start | bytes 2097152 | tf_op jit(solution)/shard_map/all_to_all | solution.py:69
  44.4 132.3 %reduce-scatter.2.cloned.1.call-start = ((), (), s32[]{:S(2)}) async-start(), calls=%async_computation.6 | async-start | bytes 3342336 | tf_op jit(solution)/shard_map/reduce_scatter | solution.py:84
  95.8 1.2 copy-start.5
  103.4 2.6 %copy-start.6 = (f32[512,768]{1,0:T(8,128)S(1)}, f32[512,768]{1,0:T(8,128)}, u32[]{:S(2)}) copy-start(f32[512,768]{1,0:T(8,128)} %copy-done.5) | copy-start | bytes 4718596
  103.4 2.6 %copy-start.7 = (f32[512,768]{1,0:T(8,128)S(1)}, f32[512,768]{1,0:T(8,128)}, u32[]{:S(2)}) copy-start(f32[512,768]{1,0:T(8,128)} %get-tuple-element.7) | copy-start | bytes 4718596
  112.3 22.1 %all-to-all-start.3 = ((bf16[32,16,1024]{2,1,0:T(8,128)(2,1)}), bf16[32,16,1024]{2,1,0:T(8,128)(2,1)S(1)}, u32[]{:S(2)}, u32[]{:S(2)}) async-start(bf16[32,16,1024]{2,1,0:T(8,128)(2,1)} %bitcast.12), calls=%async_computation.3 | async-start | bytes 2097152 | tf_op jit(solution)/shard_map/all_to_all | solution.py:94
  123.5 17.6 %copy-start.3 = (s32[128,2]{0,1:T(2,128)S(1)}, s32[128,2]{0,1:T(2,128)}, u32[]{:S(2)}) copy-start(s32[128,2]{0,1:T(2,128)} %param.13) | copy-start | bytes 3076
  134.5 20.8 %all-to-all-start.1 = ((bf16[32,16,1024]{2,1,0:T(8,128)(2,1)}), bf16[32,16,1024]{2,1,0:T(8,128)(2,1)S(1)}, u32[]{:S(2)}, u32[]{:S(2)}) async-start(bf16[32,16,1024]{2,1,0:T(8,128)(2,1)} %bitcast.7), calls=%async_computation.1 | async-start | bytes 2097152 | tf_op jit(solution)/shard_map/all_to_all | solution.py:87
  141.7 14.8 %copy-start.1 = (bf16[128,1024]{1,0:T(8,128)(2,1)S(1)}, bf16[128,1024]{1,0:T(8,128)(2,1)}, u32[]{:S(2)}) copy-start(bf16[128,1024]{1,0:T(8,128)(2,1)} %param.11) | copy-start | bytes 786436
  155.3 1.9 %copy-start.2 = (bf16[128,1024]{1,0:T(8,128)(2,1)S(1)}, bf16[128,1024]{1,0:T(8,128)(2,1)}, u32[]{:S(2)}) copy-start(bf16[128,1024]{1,0:T(8,128)(2,1)} %param.10) | copy-start | bytes 786436
Sparse Core Ops, SparseCore 0:
  10.1 83.3 all-gather.1
  103.5 73.1 reduce-scatter.1
where the time goes:
time: 186 us; the launch traced here: 185 us
  waiting for transfers between devices  104 us (56%)
  starting transfers between devices  30.1 us (16%)
  matrix products  25.9 us (14%)
  between operations  14.3 us (8%)
  other arithmetic  5.66 us (3%)
  local copies, waits for them, and re-layouts  5.32 us (3%)
    all_gather x1, waiting for transfers between devices, per_device(): mats = lax.all_gather(shards, 'dp', axis=0, tiled=True)  49 us
    reduce_scatter x1, waiting for transfers between devices, per_device(): lax.psum_scatter(partial_grad, 'dp', scatter_dimension=0, tiled=True)  18.7 us
    all_to_all x1, waiting for transfers between devices, per_device(): lax.all_to_all(out_rows.reshape(owners, capacity, feature_count), 'expert...  13.6 us
    all_to_all x1, waiting for transfers between devices, per_device(): lax.all_to_all(send_input, 'expert', split_axis=0, concat_axis=0, tiled=T...  11.6 us
    all_to_all x1, waiting for transfers between devices, per_device(): lax.all_to_all(input_cot.reshape(owners, capacity, feature_count), 'exper...  10.9 us
    all_to_all x1, starting transfers between devices, per_device(): lax.all_to_all(send_input, 'expert', split_axis=0, concat_axis=0, tiled=T...  9.51 us
    all_to_all x1, starting transfers between devices, per_device(): lax.all_to_all(input_cot.reshape(owners, capacity, feature_count), 'exper...  7.71 us
    all_to_all x1, starting transfers between devices, per_device(): lax.all_to_all(out_rows.reshape(owners, capacity, feature_count), 'expert...  6.42 us
  transfers between devices with their start and end apart: 6, of which 5 were waited for; matrix products, arithmetic and copies ran while one was open for 16% of the time, Pallas kernels for 0%

commit v1 on v0

--- a/solution.py
+++ b/solution.py
@@ -1,8 +1,22 @@
+import functools
 import math
 import jax
 import jax.numpy as jnp
 from jax import lax
 from jax.sharding import PartitionSpec as P
+
+
+def work_task_over_axis(x_in, array_axis):
+    block_last = jnp.concatenate(
+        lax.all_to_all(
+            jnp.stack([x_in for _ in range(lax.axis_size("dp"))]), "dp", split_axis=0, concat_axis=0
+        ),
+        axis=array_axis,
+    )
+    return block_last
+
+
+lay_the_skins = functools.partial(work_task_over_axis, array_axis=0)
 
 
 def expert_rows(rows_in, rows_cot, gate_mat, up_mat, down_mat):
@@ -72,7 +86,7 @@
     rows_cot = arrived_cot.reshape(slots_all, feature_count)
     hidden_count = w_gate.shape[2]
     shards = jnp.concatenate([w_gate[0], w_up[0], w_down[0]], axis=1)
-    mats = lax.all_gather(shards, "dp", axis=0, tiled=True)
+    mats = lay_the_skins(shards)
     gate_mat = mats[:, :hidden_count]
     up_mat = mats[:, hidden_count : 2 * hidden_count]
     down_mat = mats[:, 2 * hidden_count :]

time: 186 us -> 366 us (1.97)
  the two profiles are of different devices: /device:TPU:2 before, /device:TPU:14 now
where the time goes in v1:
time: 366 us; the launch traced here: 365 us
  waiting for transfers between devices  269 us (73%)
  starting transfers between devices  44.1 us (12%)
  matrix products  25.9 us (7%)
  between operations  14.3 us (4%)
  local copies, waits for them, and re-layouts  7.93 us (2%)
  other arithmetic  3.95 us (1%)
    all_to_all x1, waiting for transfers between devices, work_task_over_axis(): lax.all_to_all(jnp.stack([x_in for _ in range(lax.axis_size('dp'))]), 'dp...  203 us
    reduce_scatter x1, waiting for transfers between devices, per_device(): lax.psum_scatter(partial_grad, 'dp', scatter_dimension=0, tiled=True)  23.3 us
    all_to_all x1, waiting for transfers between devices, per_device(): lax.all_to_all(send_input, 'expert', split_axis=0, concat_axis=0, tiled=T...  13.6 us
    all_to_all x1, starting transfers between devices, work_task_over_axis(): lax.all_to_all(jnp.stack([x_in for _ in range(lax.axis_size('dp'))]), 'dp...  13.5 us
    all_to_all x1, waiting for transfers between devices, per_device(): lax.all_to_all(out_rows.reshape(owners, capacity, feature_count), 'expert...  12.9 us
    all_to_all x1, waiting for transfers between devices, per_device(): lax.all_to_all(input_cot.reshape(owners, capacity, feature_count), 'exper...  10.2 us
    all_to_all x1, starting transfers between devices, per_device(): lax.all_to_all(send_input, 'expert', split_axis=0, concat_axis=0, tiled=T...  9.46 us
  transfers between devices with their start and end apart: 6, of which 6 were waited for; matrix products, arithmetic and copies ran while one was open for 7% of the time, Pallas kernels for 0%

profile of v1, /device:TPU:14, one launch (start us, length us, event | category | flops | bytes accessed | tf_op | source)
XLA Modules:
  0.0 365.2 jit_solution(5244677446537519914)
XLA Ops:
  7.2 0.8 copy.21
  8.2 0.6 reduce-window.6
  9.2 1.2 broadcast_in_dim.6
  10.7 1.5 convolution_convert_fusion.2
  12.2 9.5 %all-to-all-start = ((bf16[32,16,1024]{2,1,0:T(8,128)(2,1)}), bf16[32,16,1024]{2,1,0:T(8,128)(2,1)S(1)}, u32[]{:S(2)}, u32[]{:S(2)}) async-start(bf16[32,16,1024]{2,1,0:T(8,128)(2,1)} %bitcast.2), calls=%async_computation | async-start | bytes 2097152 | tf_op jit(solution)/shard_map/all_to_all | solution.py:82
  21.7 13.6 %all-to-all-done = bf16[32,16,1024]{2,1,0:T(8,128)(2,1)S(1)} async-done(((bf16[32,16,1024]{2,1,0:T(8,128)(2,1)}), bf16[32,16,1024]{2,1,0:T(8,128)(2,1)S(1)}, u32[]{:S(2)}, u32[]{:S(2)}) %all-to-all-start) | async-done | bytes 1048608 | tf_op jit(solution)/shard_map/all_to_all | solution.py:82
  35.3 2.6 stack.2
  37.9 13.5 %all-to-all-start.1 = ((bf16[16,64,2304]{2,1,0:T(8,128)(2,1)}), bf16[16,64,2304]{2,1,0:T(8,128)(2,1)}, u32[]{:S(2)}, u32[]{:S(2)}) async-start(bf16[16,64,2304]{2,1,0:T(8,128)(2,1)} %stack.2), calls=%async_computation.1 | async-start | bytes 9437184 | tf_op jit(solution)/shard_map/all_to_all | solution.py:11
  51.4 0.3 broadcast_in_dim.7.clone
  51.7 0.7 convert_element_type.61
  52.7 1.6 convolution_convert_fusion.1
  54.3 202.6 %all-to-all-done.1 = bf16[16,64,2304]{2,1,0:T(8,128)(2,1)} async-done(((bf16[16,64,2304]{2,1,0:T(8,128)(2,1)}), bf16[16,64,2304]{2,1,0:T(8,128)(2,1)}, u32[]{:S(2)}, u32[]{:S(2)}) %all-to-all-start.1) | async-done | bytes 4718624 | tf_op jit(solution)/shard_map/all_to_all | solution.py:11
  256.9 6.9 %all-to-all-start.3 = ((bf16[32,16,1024]{2,1,0:T(8,128)(2,1)}), bf16[32,16,1024]{2,1,0:T(8,128)(2,1)S(1)}, u32[]{:S(2)}, u32[]{:S(2)}) async-start(bf16[32,16,1024]{2,1,0:T(8,128)(2,1)} %bitcast.11), calls=%async_computation.3 | async-start | bytes 2097152 | tf_op jit(solution)/shard_map/all_to_all | solution.py:83
  263.8 2.4 fusion.9
  266.2 1.1 copy-done.8
  267.4 3.7 %multiply_convert_fusion.2 = (bf16[512,768]{1,0:T(8,128)(2,1)S(1)}, f32[512,768]{1,0:T(8,128)}) fusion(f32[512,768]{1,0:T(8,128)S(1)} %fusion.9, bf16[512,1024]{1,0:T(8,128)(2,1)S(1)} %bitcast.55, bf16[1024,2304]{1,0:T(8,128)(2,1)} %bitcast.7), kind=kOutput, calls=%fused_computation.3 | convolution fusion | flops 807665664 | bytes 6553600 | tf_op jit(solution)/shard_map/dot_general | solution.py:24
  271.0 6.4 %all-to-all-done.3 = bf16[32,16,1024]{2,1,0:T(8,128)(2,1)S(1)} async-done(((bf16[32,16,1024]{2,1,0:T(8,128)(2,1)}), bf16[32,16,1024]{2,1,0:T(8,128)(2,1)S(1)}, u32[]{:S(2)}, u32[]{:S(2)}) %all-to-all-start.3) | async-done | bytes 1048608 | tf_op jit(solution)/shard_map/all_to_all | solution.py:83
  277.4 2.7 fusion.27
  280.1 2.5 fusion.1
  282.7 2.9 fusion.7
  285.6 3.4 add_convert_fusion
  289.1 7.1 %all-to-all-start.4 = ((bf16[32,16,1024]{2,1,0:T(8,128)(2,1)}), bf16[32,16,1024]{2,1,0:T(8,128)(2,1)S(1)}, u32[]{:S(2)}, u32[]{:S(2)}) async-start(bf16[32,16,1024]{2,1,0:T(8,128)(2,1)} %bitcast.13), calls=%async_computation.4 | async-start | bytes 2097152 | tf_op jit(solution)/shard_map/all_to_all | solution.py:108
  296.2 3.5 convolution_convert_fusion
  299.7 10.2 %all-to-all-done.4 = bf16[32,16,1024]{2,1,0:T(8,128)(2,1)S(1)} async-done(((bf16[32,16,1024]{2,1,0:T(8,128)(2,1)}), bf16[32,16,1024]{2,1,0:T(8,128)(2,1)S(1)}, u32[]{:S(2)}, u32[]{:S(2)}) %all-to-all-start.4) | async-done | bytes 1048608 | tf_op jit(solution)/shard_map/all_to_all | solution.py:108
  309.9 7.1 %all-to-all-start.2 = ((bf16[32,16,1024]{2,1,0:T(8,128)(2,1)}), bf16[32,16,1024]{2,1,0:T(8,128)(2,1)S(1)}, u32[]{:S(2)}, u32[]{:S(2)}) async-start(bf16[32,16,1024]{2,1,0:T(8,128)(2,1)} %bitcast.8), calls=%async_computation.2 | async-start | bytes 2097152 | tf_op jit(solution)/shard_map/all_to_all | solution.py:101
  317.3 0.5 convolution_reduce_fusion
  317.8 12.9 %all-to-all-done.2 = bf16[32,16,1024]{2,1,0:T(8,128)(2,1)S(1)} async-done(((bf16[32,16,1024]{2,1,0:T(8,128)(2,1)}), bf16[32,16,1024]{2,1,0:T(8,128)(2,1)S(1)}, u32[]{:S(2)}, u32[]{:S(2)}) %all-to-all-start.2) | async-done | bytes 1048608 | tf_op jit(solution)/shard_map/all_to_all | solution.py:101
  330.7 1.1 multiply_reduce_fusion
  331.9 0.8 add_convert_fusion.1
  332.7 0.8 subtract_convert_fusion
  333.4 23.3 %reduce-scatter.2.cloned.1.call-done = f32[64,768]{1,0:T(8,128)} async-done(((f32[1024,768]{1,0:T(8,128)}), f32[64,768]{1,0:T(8,128)}) %reduce-scatter.2.cloned.1.call-update) | async-done | bytes 196624 | tf_op jit(solution)/shard_map/reduce_scatter | solution.py:98
  356.8 1.6 multiply_bitcast_fusion
  (39 shorter events, 1.4 us)
Async XLA Ops:
  10.6 11.0 %copy-start.3 = (bf16[1,64,768]{2,1,0:T(8,128)(2,1)S(1)}, bf16[1,64,768]{2,1,0:T(8,128)(2,1)}, u32[]{:S(2)}) copy-start(bf16[1,64,768]{2,1,0:T(8,128)(2,1)} %param.17) | copy-start | bytes 294916
  10.6 11.0 %copy-start.4 = (bf16[1,64,768]{2,1,0:T(8,128)(2,1)S(1)}, bf16[1,64,768]{2,1,0:T(8,128)(2,1)}, u32[]{:S(2)}) copy-start(bf16[1,64,768]{2,1,0:T(8,128)(2,1)} %param.16) | copy-start | bytes 294916
  10.6 11.0 %copy-start.5 = (bf16[1,64,768]{2,1,0:T(8,128)(2,1)S(1)}, bf16[1,64,768]{2,1,0:T(8,128)(2,1)}, u32[]{:S(2)}) copy-start(bf16[1,64,768]{2,1,0:T(8,128)(2,1)} %param.15) | copy-start | bytes 294916
  12.2 23.1 %all-to-all-start = ((bf16[32,16,1024]{2,1,0:T(8,128)(2,1)}), bf16[32,16,1024]{2,1,0:T(8,128)(2,1)S(1)}, u32[]{:S(2)}, u32[]{:S(2)}) async-start(bf16[32,16,1024]{2,1,0:T(8,128)(2,1)} %bitcast.2), calls=%async_computation | async-start | bytes 2097152 | tf_op jit(solution)/shard_map/all_to_all | solution.py:82
  37.9 13.5 %copy-start = (bf16[128,1024]{1,0:T(8,128)(2,1)S(1)}, bf16[128,1024]{1,0:T(8,128)(2,1)}, u32[]{:S(2)}) copy-start(bf16[128,1024]{1,0:T(8,128)(2,1)} %param.12) | copy-start | bytes 786436
  37.9 218.9 %all-to-all-start.1 = ((bf16[16,64,2304]{2,1,0:T(8,128)(2,1)}), bf16[16,64,2304]{2,1,0:T(8,128)(2,1)}, u32[]{:S(2)}, u32[]{:S(2)}) async-start(bf16[16,64,2304]{2,1,0:T(8,128)(2,1)} %stack.2), calls=%async_computation.1 | async-start | bytes 9437184 | tf_op jit(solution)/shard_map/all_to_all | solution.py:11
  51.4 1.0 copy-start.7
  256.9 20.5 %all-to-all-start.3 = ((bf16[32,16,1024]{2,1,0:T(8,128)(2,1)}), bf16[32,16,1024]{2,1,0:T(8,128)(2,1)S(1)}, u32[]{:S(2)}, u32[]{:S(2)}) async-start(bf16[32,16,1024]{2,1,0:T(8,128)(2,1)} %bitcast.11), calls=%async_computation.3 | async-start | bytes 2097152 | tf_op jit(solution)/shard_map/all_to_all | solution.py:83
  263.8 93.0 %reduce-scatter.2.cloned.1.call-start = ((), (), s32[]{:S(2)}) async-start(), calls=%async_computation.6 | async-start | bytes 3342336 | tf_op jit(solution)/shard_map/reduce_scatter | solution.py:98
  266.2 1.1 copy-start.8
  280.1 2.6 copy-start.9
  280.1 2.6 copy-start.10
  289.1 20.9 %all-to-all-start.4 = ((bf16[32,16,1024]{2,1,0:T(8,128)(2,1)}), bf16[32,16,1024]{2,1,0:T(8,128)(2,1)S(1)}, u32[]{:S(2)}, u32[]{:S(2)}) async-start(bf16[32,16,1024]{2,1,0:T(8,128)(2,1)} %bitcast.13), calls=%async_computation.4 | async-start | bytes 2097152 | tf_op jit(solution)/shard_map/all_to_all | solution.py:108
  299.7 17.6 %copy-start.6 = (s32[128,2]{0,1:T(2,128)S(1)}, s32[128,2]{0,1:T(2,128)}, u32[]{:S(2)}) copy-start(s32[128,2]{0,1:T(2,128)} %param.13) | copy-start | bytes 3076
  309.9 20.8 %all-to-all-start.2 = ((bf16[32,16,1024]{2,1,0:T(8,128)(2,1)}), bf16[32,16,1024]{2,1,0:T(8,128)(2,1)S(1)}, u32[]{:S(2)}, u32[]{:S(2)}) async-start(bf16[32,16,1024]{2,1,0:T(8,128)(2,1)} %bitcast.8), calls=%async_computation.2 | async-start | bytes 2097152 | tf_op jit(solution)/shard_map/all_to_all | solution.py:101
  317.8 14.1 %copy-start.1 = (bf16[128,1024]{1,0:T(8,128)(2,1)S(1)}, bf16[128,1024]{1,0:T(8,128)(2,1)}, u32[]{:S(2)}) copy-start(bf16[128,1024]{1,0:T(8,128)(2,1)} %param.11) | copy-start | bytes 786436
  330.7 1.9 copy-start.2
Sparse Core Ops, SparseCore 0:
  280.2 76.4 reduce-scatter.1
